TPU v7x, 32 devices: a whole 2x2x4 slice. The times are simulated.
32 devices in a mesh: study: 2 (over y), branch: 4 (over z), scen: 2 (over x), bus: 2 (over core).
Axes of the slice: x: 2, y: 2, z: 4, core: 2. Of those that a mesh axis runs over, the one named last changes fastest.
Arguments:
- ptdf: bfloat16 [1024, 4096], P(None, ('branch', 'bus')), may hold values from -0.21875 to 0.21875
- base_flow: bfloat16 [8, 2, 32, 4096], P('study', 'scen', None, ('branch', 'bus')), parts along dimension 0, may hold values from -6 to 6
- rate_class: int32 [4096], P(('branch', 'bus')), may hold values from 0 to 15
- class_limit: float32 [16], replicated, may hold values from 0.6 to 2
- site_block: int32 [8, 2, 2, 3], P('study', 'scen'), parts along dimension 0, may hold values from 0 to 3, as said below
- profile: bfloat16 [8, 2, 2, 32, 384], P(('study', 'branch'), 'scen', 'bus'), parts along dimension 0, may hold values from 0.099609375 to 1
- size_init: float32 [8, 2, 2, 384], P(('study', 'branch'), 'scen', 'bus'), parts along dimension 0, may hold values from 0.5 to 1.5
Outputs:
- size_final: float32 [8, 2, 2, 384], P(('study', 'branch'), 'scen', 'bus'), parts along dimension 0
- flows_last: bfloat16 [8, 2, 32, 4096], P('study', 'scen', None, ('branch', 'bus')), parts along dimension 0
There are 2 independent parts, one for each index of `study`. A program takes and returns all parts, laid end to end along the dimension named above; an argument that names none is the same for every part. Nothing has to cross between parts.
Inputs may be any that keep to these rules, and one draw needn't show every extreme that they name: `site_block`: the 3 block numbers of one half of one batch's site list are distinct.
All inputs are finite; a program needn't handle non-finite values.
Results may differ from a plain program's by a relative error of at most 0.017.
Values may be sent and summed in bfloat16 or wider, within the bound.
A program may use at most 64 MiB of HBM per device.

v0:
```python
import functools
import jax
import jax.numpy as jnp
from jax import lax
from jax.experimental import pallas as pl
from jax.experimental.pallas import tpu as pltpu
from jax.sharding import PartitionSpec as P

step_length = 3.0
GROUP = ("branch", "bus")
MESH = pl.DeviceIdType.MESH


def kernel(
    n_branch, n_bus,
    ptdf_hbm, base_hbm, class_hbm, limit_hbm, block_hbm, profile_hbm, size_hbm,
    size_out, flow_out,
    limit_ref, block_ref, ptdf, base, classes, profs, sizes, later, pooled, sens, part, parts, last, lasts,
    local_sem, prof_send, prof_recv, size_send, size_recv, part_send, part_recv, last_send, last_recv,
):
    z, b = lax.axis_index("branch"), lax.axis_index("bus")
    members = n_branch * n_bus
    me = z * n_bus + b
    owners, scens, _ = base.shape
    pool = ptdf.shape[0]
    half_blocks = pool // 256
    sites = profs.shape[-1]
    slots = sites // 128

    partner = {"bus": lax.rem(b + 1, n_bus)}
    top = n_branch - 1

    def at_least(left, right):
        return (left - right + 2 * n_branch) // (2 * n_branch)

    def at(level, core):
        return level * n_bus + core

    def device(index):
        return {"branch": index // n_bus, "bus": lax.rem(index, n_bus)}

    def ahead(t):
        return lax.rem(me + t, members)

    def behind(t):
        return lax.rem(me - t + members, members)

    barrier = pltpu.get_barrier_semaphore()
    for t in range(1, members):
        pl.semaphore_signal(barrier, inc=1, device_id=device(ahead(t)), device_id_type=MESH)
    loads = [
        pltpu.make_async_copy(profile_hbm.at[0, 0, 0], profs.at[me], local_sem.at[0]),
        pltpu.make_async_copy(size_hbm.at[0, 0], sizes.at[me], local_sem.at[1]),
        pltpu.make_async_copy(class_hbm, classes, local_sem.at[2]),
        pltpu.make_async_copy(base_hbm.at[:, 0], base, local_sem.at[3]),
        pltpu.make_async_copy(ptdf_hbm, ptdf, local_sem.at[4]),
        pltpu.make_async_copy(limit_hbm, limit_ref, local_sem.at[5]),
        pltpu.make_async_copy(block_hbm, block_ref, local_sem.at[6]),
    ]
    for load in loads:
        load.start()
    loads[0].wait()
    loads[1].wait()
    pl.semaphore_wait(barrier, members - 1)

    def send(src, dst, send_sem, recv_sem, index):
        copy = pltpu.make_async_remote_copy(
            src_ref=src, dst_ref=dst, send_sem=send_sem, recv_sem=recv_sem,
            device_id=device(index), device_id_type=MESH,
        )
        copy.start()
        return copy

    def receive(dst, send_sem, recv_sem, index):
        pltpu.make_async_remote_copy(
            src_ref=dst, dst_ref=dst, send_sem=send_sem, recv_sem=recv_sem,
            device_id=device(index), device_id_type=MESH,
        ).wait_recv()

    mate = z * n_bus + lax.rem(b + 1, n_bus)
    sent = []

    def pass_on(t, index, to):
        sent.append(send(sizes.at[index], sizes.at[index], size_send, size_recv.at[index], to))
        sent.append(send(profs.at[index], profs.at[index], prof_send, prof_recv.at[index], to))

    def arrive(index):
        receive(sizes.at[index], size_send, size_recv.at[index], mate)
        receive(profs.at[index], prof_send, prof_recv.at[index], mate)

    for t in range(1, n_branch):
        pass_on(t, me, lax.rem(z + t, n_branch) * n_bus + b)
    pass_on(0, me, mate)

    loads[2].wait()
    loads[5].wait()
    loads[6].wait()
    class_row = classes[...].reshape(1, -1)
    rating = jnp.zeros(class_row.shape, jnp.float32)
    for c in range(limit_ref.shape[0]):
        rating = jnp.where(class_row == c, limit_ref[c], rating)
    inverse = 1.0 / rating
    loads[3].wait()
    loads[4].wait()

    for t in range(1, n_branch):
        index = lax.rem(z - t + n_branch, n_branch) * n_bus + b
        arrive(index)
        pass_on(n_branch - 1 + t, index, mate)
    for t in range(n_branch):
        arrive(lax.rem(z - t + n_branch, n_branch) * n_bus + lax.rem(b + 1, n_bus))

    def remote(src, dst, send_sem, recv_sem, device):
        return pltpu.make_async_remote_copy(
            src_ref=src, dst_ref=dst, send_sem=send_sem, recv_sem=recv_sem,
            device_id=device, device_id_type=MESH,
        )

    upper = z // ((n_branch + 1) // 2)

    def others():
        for i in range(top):
            k = top - i
            level = upper * (i + at_least(i, z)) + (1 - upper) * (k - at_least(z, k))
            for c in range(n_bus):
                yield at(level, lax.rem(b + c, n_bus)), {"branch": level, "bus": lax.rem(b + c, n_bus)}
        yield at(z, lax.rem(b + 1, n_bus)), partner

    def all_but_one(ref, send_sem, recv_sem):
        return remote(ref.at[pl.ds(0, members - 1)], ref.at[pl.ds(0, members - 1)], send_sem, recv_sem, partner)

    def sweep(final):
        current = later if final else sizes
        for o in range(owners):
            for h in range(2):
                j = 2 * o + h
                injected = (current[j] * profs[j].astype(jnp.float32)).astype(jnp.bfloat16).astype(jnp.float32)
                for p in range(half_blocks):
                    total = None
                    for k in range(slots):
                        hit = jnp.where(block_ref[0, k, h, o] == p, 1.0, 0.0)
                        term = injected[:, k * 128:(k + 1) * 128] * hit
                        total = term if total is None else total + term
                    at = (h * half_blocks + p) * 128
                    pooled[o * scens:(o + 1) * scens, at:at + 128] = total.astype(jnp.bfloat16)
        flow = jnp.dot(pooled[...], ptdf[...], preferred_element_type=jnp.float32)
        flow = flow + base[...].reshape(flow.shape).astype(jnp.float32)
        if final:
            flow_out[...] = flow.astype(jnp.bfloat16).reshape(flow_out.shape)
        load = flow * inverse
        adjoint = ((1.0 + jnp.tanh(0.5 * (load * load - 1.0))) * load * inverse).astype(jnp.bfloat16)
        for q in range(half_blocks):
            pair = lax.dot_general(
                adjoint, ptdf[q * 256:(q + 1) * 256, :], (((1,), (1,)), ((), ())),
                preferred_element_type=jnp.float32,
            )
            sens[2 * q] = pair[:, :128]
            sens[2 * q + 1] = pair[:, 128:]
        for o in range(owners):
            for h in range(2):
                j = 2 * o + h
                for k in range(slots):
                    rows = sens[h * half_blocks + block_ref[0, k, h, o], o * scens:(o + 1) * scens, :]
                    cut = slice(k * 128, (k + 1) * 128)
                    value = jnp.sum(rows * profs[j, :, cut].astype(jnp.float32), axis=0, keepdims=True) * (1.0 / scens)
                    if final:
                        last[j, :, cut] = value
                    else:
                        part[j:j + 1, cut] = value

    sweep(False)
    parts[me] = part[...].astype(jnp.bfloat16)
    for _, device in others():
        remote(parts.at[me], parts.at[me], part_send, part_recv, device).start()
    all_but_one(parts, part_send, part_recv).wait_recv()
    gradient = jnp.sum(parts[...].astype(jnp.float32), axis=0)
    for j in range(members):
        later[j] = sizes[j] + step_length * (1.0 - gradient[j:j + 1, :])
    sweep(True)
    for to, device in others():
        remote(last.at[to], lasts.at[me], last_send, last_recv, device).start()
    lasts[me] = last[me]
    all_but_one(parts, part_send, part_recv).wait_send()
    all_but_one(profs, prof_send, prof_recv.at[0]).wait_send()
    all_but_one(sizes, size_send, size_recv.at[0]).wait_send()
    all_but_one(lasts, last_send, last_recv).wait_recv()
    total = jnp.sum(lasts[...], axis=0)
    size_out[...] = (later[me] + step_length * (1.0 - total)).reshape(size_out.shape)
    all_but_one(lasts, last_send, last_recv).wait_send()


def per_device(n_branch, n_bus, ptdf, base_flow, rate_class, class_limit, site_block, profile, size_init):
    members = n_branch * n_bus
    owners, _, scens, rows = base_flow.shape
    pool = ptdf.shape[0]
    sites = profile.shape[-1]
    any_spec = pl.BlockSpec(memory_space=pl.ANY)
    blocks = jnp.transpose(site_block, (1, 3, 2, 0))
    vmem = pl.BlockSpec(memory_space=pltpu.VMEM)
    dma = pltpu.SemaphoreType.DMA
    return pl.pallas_call(
        functools.partial(kernel, n_branch, n_bus),
        out_shape=(
            pltpu.VMEM(size_init.shape, jnp.float32),
            pltpu.VMEM(base_flow.shape, jnp.bfloat16),
        ),
        in_specs=[any_spec] * 7,
        out_specs=(vmem, vmem),
        scratch_shapes=[
            pltpu.SMEM(class_limit.shape, jnp.float32),
            pltpu.SMEM(blocks.shape, jnp.int32),
            pltpu.VMEM(ptdf.shape, jnp.bfloat16),
            pltpu.VMEM((owners, scens, rows), jnp.bfloat16),
            pltpu.VMEM(rate_class.shape, jnp.int32),
            pltpu.VMEM((members, scens, sites), jnp.bfloat16),
            pltpu.VMEM((members, 1, sites), jnp.float32),
            pltpu.VMEM((members, 1, sites), jnp.float32),
            pltpu.VMEM((owners * scens, pool), jnp.bfloat16),
            pltpu.VMEM((pool // 128, owners * scens, 128), jnp.float32),
            pltpu.VMEM((members, sites), jnp.float32),
            pltpu.VMEM((members, members, sites), jnp.bfloat16),
            pltpu.VMEM((members, 1, sites), jnp.float32),
            pltpu.VMEM((members, 1, sites), jnp.float32),
            dma((7,)),
            dma, dma((members,)), dma, dma((members,)),
            dma, dma, dma, dma,
        ],
        compiler_params=pltpu.CompilerParams(collective_id=0, has_side_effects=True),
        name="hosting",
    )(ptdf, base_flow, rate_class, class_limit, blocks, profile, size_init)


def solution(mesh):
    in_specs = (
        P(None, ("branch", "bus")),
        P("study", "scen", None, ("branch", "bus")),
        P(("branch", "bus")),
        P(),
        P("study", "scen", None, None),
        P(("study", "branch"), "scen", "bus", None, None),
        P(("study", "branch"), "scen", "bus", None),
    )
    out_specs = (
        P(("study", "branch"), "scen", "bus", None),
        P("study", "scen", None, ("branch", "bus")),
    )
    body = functools.partial(per_device, mesh.shape["branch"], mesh.shape["bus"])
    return jax.shard_map(body, mesh=mesh, in_specs=in_specs, out_specs=out_specs, check_vma=False)
```

profile of v0, /device:TPU:0, one launch (start us, length us, event | category | flops | bytes accessed | tf_op | source)
XLA Modules:
  0.0 20.1 jit_solution(9631758521380687303)
XLA Ops:
  0.6 18.2 %hosting.1 = (f32[1,1,1,384]{3,2,1,0:T(1,128)S(1)}, bf16[4,1,32,512]{3,2,1,0:T(8,128)(2,1)S(1)}) custom-call(bf16[1024,512]{1,0:T(8,128)(2,1)} %ptdf_hbm.1, bf16[4,1,32,512]{3,2,1,0:T(8,128)(2,1)} %base_hbm.1, s32[512]{0:T(512)} %class_hbm.1, f32[16]{0:T(128)} %limit_hbm.1, s32[1,3,2,4]{3,2,1,0:T(2,128)} %bitcast.1, bf16[1,1,1,32,384]{4,3,2,1,0:T(8,128)(2,1)} %profile_hbm.1, ...), custom_call_target="tpu_custom_call" | custom-call | tf_op jit(solution)/shard_map/hosting/pallas_call | solution.py:201
  18.9 0.6 %copy.11 = f32[1,1,1,384]{3,2,1,0:T(1,128)} copy(f32[1,1,1,384]{3,2,1,0:T(1,128)S(1)} %get-tuple-element.2) | data formatting | bytes 3072
  19.4 0.7 %copy.12 = bf16[4,1,32,512]{3,2,1,0:T(8,128)(2,1)} copy(bf16[4,1,32,512]{3,2,1,0:T(8,128)(2,1)S(1)} %get-tuple-element.3) | data formatting | bytes 262144
where the time goes:
time: 20.2 us; the launch traced here: 20.1 us
  Pallas kernels  18.2 us (90%)
  local copies, waits for them, and re-layouts  1.22 us (6%)
  between operations  0.64 us (3%)
    pallas_call x1, Pallas kernels, per_device(): pl.pallas_call(functools.partial(kernel, n_branch, n_bus), out_shape=(plt...  18.2 us
    unnamed x2, local copies, waits for them, and re-layouts  1.22 us

commit v1 on v0

v1 whole, which is shorter than its diff:
```python
import functools
import jax
import jax.numpy as jnp
from jax import lax
from jax.experimental import pallas as pl
from jax.experimental.pallas import tpu as pltpu
from jax.sharding import PartitionSpec as P

step_length = 3.0
MESH = pl.DeviceIdType.MESH
FAR = 3


def kernel(
    n_branch, n_bus,
    ptdf_hbm, base_hbm, class_hbm, limit_hbm, block_hbm, profile_hbm, size_hbm,
    size_out, flow_out,
    limit_ref, block_ref, ptdf, base, classes, profs, sizes, placed, pooled, hits, later, part, parts, last, lasts,
    local_sem, ready, prof_send, prof_recv, size_send, size_recv, part_send, part_recv, last_send, last_recv,
):
    z, b = lax.axis_index("branch"), lax.axis_index("bus")
    members = n_branch * n_bus
    owners, scens, rows = base.shape
    half_blocks = ptdf.shape[0] // 256
    sites = profs.shape[-1]
    slots = sites // 128
    top = n_branch - 1
    mate = 1 - b

    def slot(level, core):
        return core * n_branch + level

    me = slot(z, b)
    upper = z // ((n_branch + 1) // 2)

    def at_least(left, right):
        return (left - right + 2 * n_branch) // (2 * n_branch)

    def farthest(i):
        k = top - i
        return upper * (i + at_least(i, z)) + (1 - upper) * (k - at_least(z, k))

    near = [farthest(top - 1 - i) for i in range(top)]

    def device(level, core):
        return {"branch": level, "bus": core}

    loads = [
        pltpu.make_async_copy(profile_hbm.at[0, 0, 0], profs.at[me], local_sem.at[0]),
        pltpu.make_async_copy(size_hbm.at[0, 0], sizes.at[me], local_sem.at[1]),
        pltpu.make_async_copy(block_hbm, block_ref, local_sem.at[6]),
        pltpu.make_async_copy(limit_hbm, limit_ref, local_sem.at[5]),
        pltpu.make_async_copy(class_hbm, classes, local_sem.at[2]),
        pltpu.make_async_copy(base_hbm.at[:, 0], base, local_sem.at[3]),
        pltpu.make_async_copy(ptdf_hbm, ptdf, local_sem.at[4]),
    ]
    loads[0].start()
    loads[1].start()

    barrier = pltpu.get_barrier_semaphore()
    for side in (-1, 1):
        level = z + side

        @pl.when((level >= 0) & (level < n_branch))
        def _():
            for core in (b, mate):
                pl.semaphore_signal(barrier, inc=1, device_id=device(level, core), device_id_type=MESH)

    pl.semaphore_signal(barrier, inc=1, device_id=device(z, mate), device_id_type=MESH)
    for load in loads[2:]:
        load.start()
    loads[0].wait()
    loads[1].wait()
    edges = jnp.where(z > 0, 1, 0) + jnp.where(z < top, 1, 0)
    pl.semaphore_wait(barrier, 1 + n_bus * edges)

    def remote(src, dst, send_sem, recv_sem, to):
        return pltpu.make_async_remote_copy(
            src_ref=src, dst_ref=dst, send_sem=send_sem, recv_sem=recv_sem,
            device_id=to, device_id_type=MESH,
        )

    def pass_on(index, to):
        remote(sizes.at[index], sizes.at[index], size_send, size_recv.at[index], to).start()
        remote(profs.at[index], profs.at[index], prof_send, prof_recv.at[index], to).start()

    def arrive(index):
        to = device(z, mate)
        remote(sizes.at[index], sizes.at[index], size_send, size_recv.at[index], to).wait_recv()
        remote(profs.at[index], profs.at[index], prof_send, prof_recv.at[index], to).wait_recv()

    def gap(level):
        return jnp.where(level > z, level - z, z - level)

    def announce(level):
        @pl.when(gap(level) > 1)
        def _():
            pl.semaphore_wait(ready.at[level], 1)

        onward = jnp.where(level > z, z - 1, z + 1)

        @pl.when((onward >= 0) & (onward < n_branch))
        def _():
            pl.semaphore_signal(ready.at[level], inc=1, device_id=device(onward, b), device_id_type=MESH)

    def offer(level):
        pass_on(me, device(level, b))

        @pl.when(gap(level) >= FAR)
        def _():
            pass_on(me, device(level, mate))

    for i, level in enumerate(near):
        announce(level)
        offer(level)
        if i == 0:
            pass_on(me, device(z, mate))

    for load in loads[2:5]:
        load.wait()
    class_row = classes[...].reshape(1, -1)
    rating = jnp.zeros(class_row.shape, jnp.float32)
    for c in range(limit_ref.shape[0]):
        rating = jnp.where(class_row == c, limit_ref[c], rating)
    inverse = 1.0 / rating
    line = lax.broadcasted_iota(jnp.int32, (members, 128), 0)
    for k in range(slots):
        number = jnp.zeros((members, 128), jnp.int32)
        for h in range(n_bus):
            for o in range(owners):
                number = jnp.where(line == slot(o, h), block_ref[0, k, h, o], number)
        for p in range(half_blocks):
            hits[p, k] = jnp.where(number == p, 1.0, 0.0)

    def place(level, core):
        index = slot(level, core)
        profile = profs[index].astype(jnp.float32)
        size = sizes[index]
        for p in range(half_blocks):
            total = weight = None
            for k in range(slots):
                hit = jnp.where(block_ref[0, k, core, level] == p, 1.0, 0.0)
                cut = slice(k * 128, (k + 1) * 128)
                term, own = profile[:, cut] * hit, size[:, cut] * hit
                total = term if total is None else total + term
                weight = own if weight is None else weight + own
            at = core * half_blocks + p
            placed[at, level] = total
            pooled[at, level] = (total * weight).astype(jnp.bfloat16)

    place(z, b)
    loads[5].wait()
    loads[6].wait()
    arrive(slot(z, mate))
    place(z, mate)
    for i, level in enumerate(near):
        index = slot(level, b)
        arrive(index)

        @pl.when(gap(level) < FAR)
        def _():
            pass_on(index, device(z, mate))

        place(level, b)
        if i > 0:
            arrive(slot(near[i - 1], mate))
            place(near[i - 1], mate)
    arrive(slot(near[-1], mate))
    place(near[-1], mate)

    def others():
        for i in range(top):
            level = farthest(i)
            for core in (b, mate):
                yield slot(level, core), device(level, core)
        yield slot(z, mate), device(z, mate)

    def all_but_one(ref, send_sem, recv_sem):
        return remote(
            ref.at[pl.ds(0, members - 1)], ref.at[pl.ds(0, members - 1)], send_sem, recv_sem, device(z, mate)
        )

    def sweep(final):
        count = owners * scens
        injected = jnp.concatenate(
            [pooled[i].reshape(count, 128) for i in range(2 * half_blocks)], axis=1
        )
        flow = jnp.dot(injected, ptdf[...], preferred_element_type=jnp.float32)
        flow = flow + base[...].reshape(flow.shape).astype(jnp.float32)
        if final:
            flow_out[...] = flow.astype(jnp.bfloat16).reshape(flow_out.shape)
        load = flow * inverse
        adjoint = ((1.0 + jnp.tanh(0.5 * (load * load - 1.0))) * load * inverse).astype(jnp.bfloat16)
        found = []
        for q in range(half_blocks):
            pair = lax.dot_general(
                adjoint, ptdf[q * 256:(q + 1) * 256, :], (((1,), (1,)), ((), ())),
                preferred_element_type=jnp.float32,
            )
            for i in range(2):
                product = pair[:, i * 128:(i + 1) * 128].reshape(owners, scens, 128) * placed[2 * q + i]
                found.append(jnp.sum(product, axis=1))
        full = [jnp.concatenate([found[p], found[half_blocks + p]], axis=0) for p in range(half_blocks)]
        values = []
        for k in range(slots):
            value = full[0] * hits[0, k]
            for p in range(1, half_blocks):
                value = value + full[p] * hits[p, k]
            values.append(value * (1.0 / scens))
        return jnp.concatenate(values, axis=1)

    parts[me] = sweep(False).astype(jnp.bfloat16)
    for _, to in others():
        remote(parts.at[me], parts.at[me], part_send, part_recv, to).start()
    all_but_one(parts, part_send, part_recv).wait_recv()
    gradient = jnp.sum(parts[...].astype(jnp.float32), axis=0)
    current = sizes[...].reshape(members, sites) + step_length * (1.0 - gradient)
    later[...] = current
    for p in range(half_blocks):
        weight = current[:, :128] * hits[p, 0]
        for k in range(1, slots):
            weight = weight + current[:, k * 128:(k + 1) * 128] * hits[p, k]
        for h in range(2):
            for o in range(owners):
                at = h * half_blocks + p
                r = slot(o, h)
                pooled[at, o] = (placed[at, o] * weight[r:r + 1]).astype(jnp.bfloat16)
    last[...] = sweep(True).reshape(last.shape)
    for to, where in others():
        remote(last.at[to], lasts.at[me], last_send, last_recv, where).start()
    lasts[me] = last[me]
    all_but_one(parts, part_send, part_recv).wait_send()
    all_but_one(profs, prof_send, prof_recv.at[0]).wait_send()
    all_but_one(sizes, size_send, size_recv.at[0]).wait_send()
    all_but_one(lasts, last_send, last_recv).wait_recv()
    total = jnp.sum(lasts[...], axis=0)
    size_out[...] = (later[pl.ds(me, 1), :] + step_length * (1.0 - total)).reshape(size_out.shape)
    all_but_one(lasts, last_send, last_recv).wait_send()


def per_device(n_branch, n_bus, ptdf, base_flow, rate_class, class_limit, site_block, profile, size_init):
    members = n_branch * n_bus
    owners, _, scens, rows = base_flow.shape
    pool = ptdf.shape[0]
    sites = profile.shape[-1]
    any_spec = pl.BlockSpec(memory_space=pl.ANY)
    blocks = jnp.transpose(site_block, (1, 3, 2, 0))
    vmem = pl.BlockSpec(memory_space=pltpu.VMEM)
    dma = pltpu.SemaphoreType.DMA
    return pl.pallas_call(
        functools.partial(kernel, n_branch, n_bus),
        out_shape=(
            pltpu.VMEM(size_init.shape, jnp.float32),
            pltpu.VMEM(base_flow.shape, jnp.bfloat16),
        ),
        in_specs=[any_spec] * 7,
        out_specs=(vmem, vmem),
        scratch_shapes=[
            pltpu.SMEM(class_limit.shape, jnp.float32),
            pltpu.SMEM(blocks.shape, jnp.int32),
            pltpu.VMEM(ptdf.shape, jnp.bfloat16),
            pltpu.VMEM((owners, scens, rows), jnp.bfloat16),
            pltpu.VMEM(rate_class.shape, jnp.int32),
            pltpu.VMEM((members, scens, sites), jnp.bfloat16),
            pltpu.VMEM((members, 1, sites), jnp.float32),
            pltpu.VMEM((pool // 128, owners, scens, 128), jnp.float32),
            pltpu.VMEM((pool // 128, owners, scens, 128), jnp.bfloat16),
            pltpu.VMEM((pool // 256, sites // 128, members, 128), jnp.float32),
            pltpu.VMEM((members, sites), jnp.float32),
            pltpu.VMEM((members, sites), jnp.float32),
            pltpu.VMEM((members, members, sites), jnp.bfloat16),
            pltpu.VMEM((members, 1, sites), jnp.float32),
            pltpu.VMEM((members, 1, sites), jnp.float32),
            dma((7,)), pltpu.SemaphoreType.REGULAR((n_branch,)),
            dma, dma((members,)), dma, dma((members,)),
            dma, dma, dma, dma,
        ],
        compiler_params=pltpu.CompilerParams(collective_id=0, has_side_effects=True),
        name="hosting",
    )(ptdf, base_flow, rate_class, class_limit, blocks, profile, size_init)


def solution(mesh):
    in_specs = (
        P(None, ("branch", "bus")),
        P("study", "scen", None, ("branch", "bus")),
        P(("branch", "bus")),
        P(),
        P("study", "scen", None, None),
        P(("study", "branch"), "scen", "bus", None, None),
        P(("study", "branch"), "scen", "bus", None),
    )
    out_specs = (
        P(("study", "branch"), "scen", "bus", None),
        P("study", "scen", None, ("branch", "bus")),
    )
    body = functools.partial(per_device, mesh.shape["branch"], mesh.shape["bus"])
    return jax.shard_map(body, mesh=mesh, in_specs=in_specs, out_specs=out_specs, check_vma=False)
```

time: 20.2 us -> 20.6 us (1.020)
  Pallas kernels: 18.2 us -> 18.6 us
    pallas_call x1, Pallas kernels: 18.2 us -> 18.6 us  [per_device(): pl.pallas_call(functools.partial(kernel, n_branch, n_bus), out_shape=(plt...]
where the time goes in v1:
time: 20.6 us; the launch traced here: 20.5 us
  Pallas kernels  18.6 us (90%)
  local copies, waits for them, and re-layouts  1.22 us (6%)
  between operations  0.64 us (3%)
    pallas_call x1, Pallas kernels, per_device(): pl.pallas_call(functools.partial(kernel, n_branch, n_bus), out_shape=(plt...  18.6 us
    unnamed x2, local copies, waits for them, and re-layouts  1.22 us

profile of v1, /device:TPU:0, one launch (start us, length us, event | category | flops | bytes accessed | tf_op | source)
XLA Modules:
  0.0 20.5 jit_solution(7003472831587390611)
XLA Ops:
  0.6 18.6 %hosting.1 = (f32[1,1,1,384]{3,2,1,0:T(1,128)S(1)}, bf16[4,1,32,512]{3,2,1,0:T(8,128)(2,1)S(1)}) custom-call(bf16[1024,512]{1,0:T(8,128)(2,1)} %ptdf_hbm.1, bf16[4,1,32,512]{3,2,1,0:T(8,128)(2,1)} %base_hbm.1, s32[512]{0:T(512)} %class_hbm.1, f32[16]{0:T(128)} %limit_hbm.1, s32[1,3,2,4]{3,2,1,0:T(2,128)} %bitcast.1, bf16[1,1,1,32,384]{4,3,2,1,0:T(8,128)(2,1)} %profile_hbm.1, ...), custom_call_target="tpu_custom_call" | custom-call | tf_op jit(solution)/shard_map/hosting/pallas_call | solution.py:250
  19.2 0.6 %copy.11 = f32[1,1,1,384]{3,2,1,0:T(1,128)} copy(f32[1,1,1,384]{3,2,1,0:T(1,128)S(1)} %get-tuple-element.2) | data formatting | bytes 3072
  19.8 0.7 %copy.12 = bf16[4,1,32,512]{3,2,1,0:T(8,128)(2,1)} copy(bf16[4,1,32,512]{3,2,1,0:T(8,128)(2,1)S(1)} %get-tuple-element.3) | data formatting | bytes 262144

commit v2 on v0

--- a/solution.py
+++ b/solution.py
@@ -189,6 +189,17 @@
     all_but_one(lasts, last_send, last_recv).wait_send()
 
 
+def writer(size_ref, flow_ref, size_hbm, flow_hbm, sems):
+    copies = [
+        pltpu.make_async_copy(flow_ref, flow_hbm, sems.at[0]),
+        pltpu.make_async_copy(size_ref, size_hbm, sems.at[1]),
+    ]
+    for copy in copies:
+        copy.start()
+    for copy in copies:
+        copy.wait()
+
+
 def per_device(n_branch, n_bus, ptdf, base_flow, rate_class, class_limit, site_block, profile, size_init):
     members = n_branch * n_bus
     owners, _, scens, rows = base_flow.shape
@@ -198,7 +209,7 @@
     blocks = jnp.transpose(site_block, (1, 3, 2, 0))
     vmem = pl.BlockSpec(memory_space=pltpu.VMEM)
     dma = pltpu.SemaphoreType.DMA
-    return pl.pallas_call(
+    size, flow = pl.pallas_call(
         functools.partial(kernel, n_branch, n_bus),
         out_shape=(
             pltpu.VMEM(size_init.shape, jnp.float32),
@@ -228,6 +239,18 @@
         compiler_params=pltpu.CompilerParams(collective_id=0, has_side_effects=True),
         name="hosting",
     )(ptdf, base_flow, rate_class, class_limit, blocks, profile, size_init)
+    size, flow = [pltpu.with_memory_space_constraint(v, pltpu.VMEM) for v in (size, flow)]
+    return pl.pallas_call(
+        writer,
+        out_shape=(
+            jax.ShapeDtypeStruct(size_init.shape, jnp.float32),
+            jax.ShapeDtypeStruct(base_flow.shape, jnp.bfloat16),
+        ),
+        in_specs=[any_spec, any_spec],
+        out_specs=(any_spec, any_spec),
+        scratch_shapes=[dma((2,))],
+        name="writer",
+    )(size, flow)
 
 
 def solution(mesh):

time: 20.2 us -> 19.7 us (0.975)
  local copies, waits for them, and re-layouts: 1.22 us -> 0 us
  Pallas kernels: 18.2 us -> 18.9 us
    unnamed x2 -> x0, local copies, waits for them, and re-layouts: 1.22 us -> none
    pallas_call x0 -> x1, Pallas kernels: none -> 0.68 us  [per_device(): pl.pallas_call(writer, out_shape=(jax.ShapeDtypeStruct(size_init.shape, j...]
where the time goes in v2:
time: 19.7 us; the launch traced here: 19.5 us
  Pallas kernels  18.9 us (96%)
  between operations  0.64 us (3%)
    pallas_call x1, Pallas kernels, per_device(): pl.pallas_call(functools.partial(kernel, n_branch, n_bus), out_shape=(plt...  18.2 us
    pallas_call x1, Pallas kernels, per_device(): pl.pallas_call(writer, out_shape=(jax.ShapeDtypeStruct(size_init.shape, j...  0.68 us

profile of v2, /device:TPU:0, one launch (start us, length us, event | category | flops | bytes accessed | tf_op | source)
XLA Modules:
  0.0 19.5 jit_solution(14356387375899679944)
XLA Ops:
  0.6 18.2 %hosting.1 = (f32[1,1,1,384]{3,2,1,0:T(1,128)S(1)}, bf16[4,1,32,512]{3,2,1,0:T(8,128)(2,1)S(1)}) custom-call(bf16[1024,512]{1,0:T(8,128)(2,1)} %ptdf_hbm.1, bf16[4,1,32,512]{3,2,1,0:T(8,128)(2,1)} %base_hbm.1, s32[512]{0:T(512)} %class_hbm.1, f32[16]{0:T(128)} %limit_hbm.1, s32[1,3,2,4]{3,2,1,0:T(2,128)} %bitcast.1, bf16[1,1,1,32,384]{4,3,2,1,0:T(8,128)(2,1)} %profile_hbm.1, ...), custom_call_target="tpu_custom_call" | custom-call | tf_op jit(solution)/shard_map/hosting/pallas_call | solution.py:212
  18.9 0.7 %writer.1 = (f32[1,1,1,384]{3,2,1,0:T(1,128)}, bf16[4,1,32,512]{3,2,1,0:T(8,128)(2,1)}) custom-call(f32[1,1,1,384]{3,2,1,0:T(1,128)S(1)} %get-tuple-element.4.size_ref, bf16[4,1,32,512]{3,2,1,0:T(8,128)(2,1)S(1)} %get-tuple-element.5.flow_ref), custom_call_target="tpu_custom_call" | custom-call | tf_op jit(solution)/shard_map/writer/pallas_call | solution.py:243

commit v3 on v1

--- a/solution.py
+++ b/solution.py
@@ -8,15 +8,14 @@
 
 step_length = 3.0
 MESH = pl.DeviceIdType.MESH
-FAR = 3
 
 
 def kernel(
     n_branch, n_bus,
     ptdf_hbm, base_hbm, class_hbm, limit_hbm, block_hbm, profile_hbm, size_hbm,
     size_out, flow_out,
-    limit_ref, block_ref, ptdf, base, classes, profs, sizes, placed, pooled, hits, later, part, parts, last, lasts,
-    local_sem, ready, prof_send, prof_recv, size_send, size_recv, part_send, part_recv, last_send, last_recv,
+    limit_ref, block_ref, ptdf, base, classes, profs, sizes, placed, pooled, hits, weights, partial, later, parts, last, lasts,
+    local_sem, prof_send, prof_recv, size_send, size_recv, part_send, part_recv, last_send, last_recv,
 ):
     z, b = lax.axis_index("branch"), lax.axis_index("bus")
     members = n_branch * n_bus
@@ -58,21 +57,16 @@
     loads[1].start()
 
     barrier = pltpu.get_barrier_semaphore()
-    for side in (-1, 1):
-        level = z + side
-
-        @pl.when((level >= 0) & (level < n_branch))
-        def _():
-            for core in (b, mate):
-                pl.semaphore_signal(barrier, inc=1, device_id=device(level, core), device_id_type=MESH)
-
+    for i in range(top):
+        level = farthest(i)
+        for core in (b, mate):
+            pl.semaphore_signal(barrier, inc=1, device_id=device(level, core), device_id_type=MESH)
     pl.semaphore_signal(barrier, inc=1, device_id=device(z, mate), device_id_type=MESH)
     for load in loads[2:]:
         load.start()
     loads[0].wait()
     loads[1].wait()
-    edges = jnp.where(z > 0, 1, 0) + jnp.where(z < top, 1, 0)
-    pl.semaphore_wait(barrier, 1 + n_bus * edges)
+    pl.semaphore_wait(barrier, members - 1)
 
     def remote(src, dst, send_sem, recv_sem, to):
         return pltpu.make_async_remote_copy(
@@ -81,40 +75,18 @@
         )
 
     def pass_on(index, to):
-        remote(sizes.at[index], sizes.at[index], size_send, size_recv.at[index], to).start()
         remote(profs.at[index], profs.at[index], prof_send, prof_recv.at[index], to).start()
 
     def arrive(index):
-        to = device(z, mate)
-        remote(sizes.at[index], sizes.at[index], size_send, size_recv.at[index], to).wait_recv()
-        remote(profs.at[index], profs.at[index], prof_send, prof_recv.at[index], to).wait_recv()
-
-    def gap(level):
-        return jnp.where(level > z, level - z, z - level)
-
-    def announce(level):
-        @pl.when(gap(level) > 1)
-        def _():
-            pl.semaphore_wait(ready.at[level], 1)
-
-        onward = jnp.where(level > z, z - 1, z + 1)
-
-        @pl.when((onward >= 0) & (onward < n_branch))
-        def _():
-            pl.semaphore_signal(ready.at[level], inc=1, device_id=device(onward, b), device_id_type=MESH)
-
-    def offer(level):
+        remote(profs.at[index], profs.at[index], prof_send, prof_recv.at[index], device(z, mate)).wait_recv()
+
+    for level in near[::-1]:
         pass_on(me, device(level, b))
-
-        @pl.when(gap(level) >= FAR)
-        def _():
-            pass_on(me, device(level, mate))
-
-    for i, level in enumerate(near):
-        announce(level)
-        offer(level)
-        if i == 0:
-            pass_on(me, device(z, mate))
+    for level in near[::-1]:
+        for core in (b, mate):
+            remote(sizes.at[me], sizes.at[me], size_send, size_recv, device(level, core)).start()
+    remote(sizes.at[me], sizes.at[me], size_send, size_recv, device(z, mate)).start()
+    pass_on(me, device(z, mate))
 
     for load in loads[2:5]:
         load.wait()
@@ -132,41 +104,59 @@
         for p in range(half_blocks):
             hits[p, k] = jnp.where(number == p, 1.0, 0.0)
 
+    def all_but_one(ref, send_sem, recv_sem):
+        return remote(
+            ref.at[pl.ds(0, members - 1)], ref.at[pl.ds(0, members - 1)], send_sem, recv_sem, device(z, mate)
+        )
+
     def place(level, core):
-        index = slot(level, core)
-        profile = profs[index].astype(jnp.float32)
-        size = sizes[index]
+        profile = profs[slot(level, core)].astype(jnp.float32)
         for p in range(half_blocks):
-            total = weight = None
+            total = None
             for k in range(slots):
-                hit = jnp.where(block_ref[0, k, core, level] == p, 1.0, 0.0)
-                cut = slice(k * 128, (k + 1) * 128)
-                term, own = profile[:, cut] * hit, size[:, cut] * hit
+                term = profile[:, k * 128:(k + 1) * 128] * jnp.where(block_ref[0, k, core, level] == p, 1.0, 0.0)
                 total = term if total is None else total + term
-                weight = own if weight is None else weight + own
+            placed[core * half_blocks + p, level] = total
+
+    def weigh(level, core):
+        for p in range(half_blocks):
             at = core * half_blocks + p
-            placed[at, level] = total
-            pooled[at, level] = (total * weight).astype(jnp.bfloat16)
+            weight = weights[p, pl.ds(slot(level, core), 1), :]
+            pooled[at, level] = (placed[at, level] * weight).astype(jnp.bfloat16)
+
+    def spread(current):
+        for p in range(half_blocks):
+            weight = current[:, :128] * hits[p, 0]
+            for k in range(1, slots):
+                weight = weight + current[:, k * 128:(k + 1) * 128] * hits[p, k]
+            weights[p] = weight
+
+    def half_flow(core):
+        count = owners * scens
+        injected = jnp.concatenate(
+            [pooled[core * half_blocks + i].reshape(count, 128) for i in range(half_blocks)], axis=1
+        )
+        depth = half_blocks * 128
+        used = ptdf[pl.ds(pl.multiple_of(core * depth, depth), depth), :]
+        return jnp.dot(injected, used, preferred_element_type=jnp.float32)
 
     place(z, b)
+    for level in near:
+        arrive(slot(level, b))
+        pass_on(slot(level, b), device(z, mate))
+        place(level, b)
+    all_but_one(sizes, size_send, size_recv).wait_recv()
+    spread(sizes[...].reshape(members, sites))
+    for level in [z] + near:
+        weigh(level, b)
     loads[5].wait()
     loads[6].wait()
-    arrive(slot(z, mate))
-    place(z, mate)
-    for i, level in enumerate(near):
-        index = slot(level, b)
-        arrive(index)
-
-        @pl.when(gap(level) < FAR)
-        def _():
-            pass_on(index, device(z, mate))
-
-        place(level, b)
-        if i > 0:
-            arrive(slot(near[i - 1], mate))
-            place(near[i - 1], mate)
-    arrive(slot(near[-1], mate))
-    place(near[-1], mate)
+    half = half_flow(b)
+    partial[...] = half + base[...].reshape(half.shape).astype(jnp.float32)
+    for level in [z] + near:
+        arrive(slot(level, mate))
+        place(level, mate)
+        weigh(level, mate)
 
     def others():
         for i in range(top):
@@ -175,18 +165,16 @@
                 yield slot(level, core), device(level, core)
         yield slot(z, mate), device(z, mate)
 
-    def all_but_one(ref, send_sem, recv_sem):
-        return remote(
-            ref.at[pl.ds(0, members - 1)], ref.at[pl.ds(0, members - 1)], send_sem, recv_sem, device(z, mate)
-        )
-
     def sweep(final):
-        count = owners * scens
-        injected = jnp.concatenate(
-            [pooled[i].reshape(count, 128) for i in range(2 * half_blocks)], axis=1
-        )
-        flow = jnp.dot(injected, ptdf[...], preferred_element_type=jnp.float32)
-        flow = flow + base[...].reshape(flow.shape).astype(jnp.float32)
+        if final:
+            count = owners * scens
+            injected = jnp.concatenate(
+                [pooled[i].reshape(count, 128) for i in range(2 * half_blocks)], axis=1
+            )
+            flow = jnp.dot(injected, ptdf[...], preferred_element_type=jnp.float32)
+            flow = flow + base[...].reshape(flow.shape).astype(jnp.float32)
+        else:
+            flow = partial[...] + half_flow(mate)
         if final:
             flow_out[...] = flow.astype(jnp.bfloat16).reshape(flow_out.shape)
         load = flow * inverse
@@ -231,11 +219,22 @@
     lasts[me] = last[me]
     all_but_one(parts, part_send, part_recv).wait_send()
     all_but_one(profs, prof_send, prof_recv.at[0]).wait_send()
-    all_but_one(sizes, size_send, size_recv.at[0]).wait_send()
+    all_but_one(sizes, size_send, size_recv).wait_send()
     all_but_one(lasts, last_send, last_recv).wait_recv()
     total = jnp.sum(lasts[...], axis=0)
     size_out[...] = (later[pl.ds(me, 1), :] + step_length * (1.0 - total)).reshape(size_out.shape)
     all_but_one(lasts, last_send, last_recv).wait_send()
+
+
+def writer(size_ref, flow_ref, size_hbm, flow_hbm, sems):
+    copies = [
+        pltpu.make_async_copy(flow_ref, flow_hbm, sems.at[0]),
+        pltpu.make_async_copy(size_ref, size_hbm, sems.at[1]),
+    ]
+    for copy in copies:
+        copy.start()
+    for copy in copies:
+        copy.wait()
 
 
 def per_device(n_branch, n_bus, ptdf, base_flow, rate_class, class_limit, site_block, profile, size_init):
@@ -247,7 +246,7 @@
     blocks = jnp.transpose(site_block, (1, 3, 2, 0))
     vmem = pl.BlockSpec(memory_space=pltpu.VMEM)
     dma = pltpu.SemaphoreType.DMA
-    return pl.pallas_call(
+    size, flow = pl.pallas_call(
         functools.partial(kernel, n_branch, n_bus),
         out_shape=(
             pltpu.VMEM(size_init.shape, jnp.float32),
@@ -266,18 +265,31 @@
             pltpu.VMEM((pool // 128, owners, scens, 128), jnp.float32),
             pltpu.VMEM((pool // 128, owners, scens, 128), jnp.bfloat16),
             pltpu.VMEM((pool // 256, sites // 128, members, 128), jnp.float32),
-            pltpu.VMEM((members, sites), jnp.float32),
+            pltpu.VMEM((pool // 256, members, 128), jnp.float32),
+            pltpu.VMEM((owners * scens, rows), jnp.float32),
             pltpu.VMEM((members, sites), jnp.float32),
             pltpu.VMEM((members, members, sites), jnp.bfloat16),
             pltpu.VMEM((members, 1, sites), jnp.float32),
             pltpu.VMEM((members, 1, sites), jnp.float32),
-            dma((7,)), pltpu.SemaphoreType.REGULAR((n_branch,)),
-            dma, dma((members,)), dma, dma((members,)),
+            dma((7,)),
+            dma, dma((members,)), dma, dma,
             dma, dma, dma, dma,
         ],
         compiler_params=pltpu.CompilerParams(collective_id=0, has_side_effects=True),
         name="hosting",
     )(ptdf, base_flow, rate_class, class_limit, blocks, profile, size_init)
+    size, flow = [pltpu.with_memory_space_constraint(v, pltpu.VMEM) for v in (size, flow)]
+    return pl.pallas_call(
+        writer,
+        out_shape=(
+            jax.ShapeDtypeStruct(size_init.shape, jnp.float32),
+            jax.ShapeDtypeStruct(base_flow.shape, jnp.bfloat16),
+        ),
+        in_specs=[any_spec, any_spec],
+        out_specs=(any_spec, any_spec),
+        scratch_shapes=[dma((2,))],
+        name="writer",
+    )(size, flow)
 
 
 def solution(mesh):

time: 20.6 us -> 19.4 us (0.942)
  local copies, waits for them, and re-layouts: 1.22 us -> 0 us
    unnamed x2 -> x0, local copies, waits for them, and re-layouts: 1.22 us -> none
    pallas_call x1, Pallas kernels: 18.6 us -> 17.9 us  [per_device(): pl.pallas_call(functools.partial(kernel, n_branch, n_bus), out_shape=(plt...]
    pallas_call x0 -> x1, Pallas kernels: none -> 0.68 us  [per_device(): pl.pallas_call(writer, out_shape=(jax.ShapeDtypeStruct(size_init.shape, j...]
where the time goes in v3:
time: 19.4 us; the launch traced here: 19.2 us
  Pallas kernels  18.6 us (96%)
  between operations  0.64 us (3%)
    pallas_call x1, Pallas kernels, per_device(): pl.pallas_call(functools.partial(kernel, n_branch, n_bus), out_shape=(plt...  17.9 us
    pallas_call x1, Pallas kernels, per_device(): pl.pallas_call(writer, out_shape=(jax.ShapeDtypeStruct(size_init.shape, j...  0.68 us

profile of v3, /device:TPU:0, one launch (start us, length us, event | category | flops | bytes accessed | tf_op | source)
XLA Modules:
  0.0 19.2 jit_solution(7437866071693805158)
XLA Ops:
  0.6 17.9 %hosting.1 = (f32[1,1,1,384]{3,2,1,0:T(1,128)S(1)}, bf16[4,1,32,512]{3,2,1,0:T(8,128)(2,1)S(1)}) custom-call(bf16[1024,512]{1,0:T(8,128)(2,1)} %ptdf_hbm.1, bf16[4,1,32,512]{3,2,1,0:T(8,128)(2,1)} %base_hbm.1, s32[512]{0:T(512)} %class_hbm.1, f32[16]{0:T(128)} %limit_hbm.1, s32[1,3,2,4]{3,2,1,0:T(2,128)} %bitcast.1, bf16[1,1,1,32,384]{4,3,2,1,0:T(8,128)(2,1)} %profile_hbm.1, ...), custom_call_target="tpu_custom_call" | custom-call | tf_op jit(solution)/shard_map/hosting/pallas_call | solution.py:249
  18.6 0.7 %writer.1 = (f32[1,1,1,384]{3,2,1,0:T(1,128)}, bf16[4,1,32,512]{3,2,1,0:T(8,128)(2,1)}) custom-call(f32[1,1,1,384]{3,2,1,0:T(1,128)S(1)} %get-tuple-element.4.size_ref, bf16[4,1,32,512]{3,2,1,0:T(8,128)(2,1)S(1)} %get-tuple-element.5.flow_ref), custom_call_target="tpu_custom_call" | custom-call | tf_op jit(solution)/shard_map/writer/pallas_call | solution.py:282

commit v4 on v3

--- a/solution.py
+++ b/solution.py
@@ -177,14 +177,23 @@
             flow = partial[...] + half_flow(mate)
         if final:
             flow_out[...] = flow.astype(jnp.bfloat16).reshape(flow_out.shape)
-        load = flow * inverse
-        adjoint = ((1.0 + jnp.tanh(0.5 * (load * load - 1.0))) * load * inverse).astype(jnp.bfloat16)
+        wide = rows // 2
+        adjoints = []
+        for c in range(2):
+            side = slice(c * wide, (c + 1) * wide)
+            load = flow[:, side] * inverse[:, side]
+            adjoints.append(
+                ((1.0 + jnp.tanh(0.5 * (load * load - 1.0))) * load * inverse[:, side]).astype(jnp.bfloat16)
+            )
         found = []
         for q in range(half_blocks):
-            pair = lax.dot_general(
-                adjoint, ptdf[q * 256:(q + 1) * 256, :], (((1,), (1,)), ((), ())),
-                preferred_element_type=jnp.float32,
-            )
+            pair = None
+            for c in range(2):
+                term = lax.dot_general(
+                    adjoints[c], ptdf[q * 256:(q + 1) * 256, c * wide:(c + 1) * wide], (((1,), (1,)), ((), ())),
+                    preferred_element_type=jnp.float32,
+                )
+                pair = term if pair is None else pair + term
             for i in range(2):
                 product = pair[:, i * 128:(i + 1) * 128].reshape(owners, scens, 128) * placed[2 * q + i]
                 found.append(jnp.sum(product, axis=1))

time: 19.4 us -> 19.4 us (level)
  no operation moved by 1% of the time
where the time goes in v4:
time: 19.4 us; the launch traced here: 19.2 us
  Pallas kernels  18.6 us (96%)
  between operations  0.64 us (3%)
    pallas_call x1, Pallas kernels, per_device(): pl.pallas_call(functools.partial(kernel, n_branch, n_bus), out_shape=(plt...  17.9 us
    pallas_call x1, Pallas kernels, per_device(): pl.pallas_call(writer, out_shape=(jax.ShapeDtypeStruct(size_init.shape, j...  0.68 us

profile of v4, /device:TPU:0, one launch (start us, length us, event | category | flops | bytes accessed | tf_op | source)
XLA Modules:
  0.0 19.2 jit_solution(12212624445024567610)
XLA Ops:
  0.6 17.9 %hosting.1 = (f32[1,1,1,384]{3,2,1,0:T(1,128)S(1)}, bf16[4,1,32,512]{3,2,1,0:T(8,128)(2,1)S(1)}) custom-call(bf16[1024,512]{1,0:T(8,128)(2,1)} %ptdf_hbm.1, bf16[4,1,32,512]{3,2,1,0:T(8,128)(2,1)} %base_hbm.1, s32[512]{0:T(512)} %class_hbm.1, f32[16]{0:T(128)} %limit_hbm.1, s32[1,3,2,4]{3,2,1,0:T(2,128)} %bitcast.1, bf16[1,1,1,32,384]{4,3,2,1,0:T(8,128)(2,1)} %profile_hbm.1, ...), custom_call_target="tpu_custom_call" | custom-call | tf_op jit(solution)/shard_map/hosting/pallas_call | solution.py:258
  18.5 0.7 %writer.1 = (f32[1,1,1,384]{3,2,1,0:T(1,128)}, bf16[4,1,32,512]{3,2,1,0:T(8,128)(2,1)}) custom-call(f32[1,1,1,384]{3,2,1,0:T(1,128)S(1)} %get-tuple-element.4.size_ref, bf16[4,1,32,512]{3,2,1,0:T(8,128)(2,1)S(1)} %get-tuple-element.5.flow_ref), custom_call_target="tpu_custom_call" | custom-call | tf_op jit(solution)/shard_map/writer/pallas_call | solution.py:291
